TPU v7x, 32 devices: a whole 2x2x4 slice. The times are simulated.
32 devices in a mesh: section: 2 (over x), dp: 16 (over z, y, core).
Axes of the slice: x: 2, y: 2, z: 4, core: 2. Of those that a mesh axis runs over, the one named last changes fastest.
Arguments:
- section_inputs: bfloat16 [2, 2048, 8192], P('section', 'dp'), may hold values from -6 to 6
- teacher_states: bfloat16 [2048, 8192], P('dp'), may hold values from -6 to 6
- confidence: int32 [2048], P('dp'), may hold values from 1 to 256
- gains: float32 [2, 8192], P('section'), may hold values from 0.1 to 1.9
- w_down: bfloat16 [2, 8192, 256], P('section', 'dp'), may hold values from -0.0625 to 0.0625
- w_up: bfloat16 [2, 8192, 256], P('section', 'dp'), may hold values from -0.375 to 0.375
Outputs:
- input_grads: bfloat16 [2, 2048, 8192], P('section', 'dp')
- grad_down: float32 [2, 8192, 256], P('section', 'dp')
- grad_up: float32 [2, 8192, 256], P('section', 'dp')
- grad_gain: float32 [2, 8192], P('section', 'dp')
All inputs are finite; a program needn't handle non-finite values.
Results may differ from a plain program's by a relative error of at most 0.013.
Values may be sent and summed in bfloat16 or wider, within the bound.
No kernel may reach another device: no remote copies, remote signals or barrier semaphores. Data moves between devices by JAX's collectives and lax.ppermute only.
A program may use at most 64 MiB of HBM per device.

v0:
```python
import jax
import jax.numpy as jnp
from jax import lax
from jax.sharding import PartitionSpec as P

MICRO = 4
ROWS = 32
TOK_DEV = 128
EPSILON = 1e-05


def shifted(block, axis, distance):
    devices = range(lax.axis_size(axis))
    route = [(i - distance, i) for i in devices if i - distance in devices]
    return lax.ppermute(block, axis, route)


def write_rows(buffer, fresh, first_row, active_step):
    previous = lax.dynamic_slice_in_dim(buffer, first_row, fresh.shape[0], 0)
    return lax.dynamic_update_slice_in_dim(
        buffer, jnp.where(active_step, fresh, previous), first_row, 0
    )


def local(section_inputs, teacher_states, confidence, gains, w_down, w_up):
    sections = lax.axis_size("section")
    section_index = lax.axis_index("section")
    layer_inputs = section_inputs[0]
    gain = gains[0]
    down_matrix, up_matrix = (
        lax.all_gather(w_down[0], "dp", axis=0, tiled=True),
        lax.all_gather(w_up[0], "dp", axis=0, tiled=True),
    )
    is_last = section_index == sections - 1
    rank_width = down_matrix.shape[1]
    width = down_matrix.shape[0]

    def run_step(step_index, carry):
        incoming, scaled_all, cot_all, pre_all, hidden_all, grads_all, gain_term = carry
        micro_index = step_index - (sections - 1 - section_index)
        active_step = (micro_index >= 0) & (micro_index < MICRO)
        first_row = jnp.clip(micro_index, 0, MICRO - 1) * ROWS
        rows_in = lax.dynamic_slice_in_dim(layer_inputs, first_row, ROWS, 0)
        teacher_rows = lax.dynamic_slice_in_dim(teacher_states, first_row, ROWS, 0)
        weight_rows = (
            lax.dynamic_slice_in_dim(confidence, first_row, ROWS, 0).astype(jnp.float32) / 256.0
        )
        values = rows_in.astype(jnp.float32)
        inverse = lax.rsqrt(jnp.mean(values * values, axis=-1, keepdims=True) + EPSILON)
        normed = values * inverse
        scaled = (normed * gain).astype(jnp.bfloat16)
        preact = jnp.dot(scaled, down_matrix, preferred_element_type=jnp.float32)
        hidden = jax.nn.silu(preact).astype(jnp.bfloat16)
        branch = jnp.einsum("tr,dr->td", hidden, up_matrix, preferred_element_type=jnp.float32)
        top_grad = (
            weight_rows[:, None] * (values + branch - teacher_rows.astype(jnp.float32))
        ).astype(jnp.bfloat16)
        cotangent = jnp.where(is_last, top_grad, incoming)
        hidden_grad = jnp.dot(cotangent, up_matrix, preferred_element_type=jnp.float32)
        sigmoid_val = jax.nn.sigmoid(preact)
        pre_grad = (hidden_grad * sigmoid_val * (1.0 + preact * (1.0 - sigmoid_val))).astype(
            jnp.bfloat16
        )
        normed_grad = jnp.einsum(
            "tr,dr->td", pre_grad, down_matrix, preferred_element_type=jnp.float32
        )
        scaled_grad = normed_grad * gain
        input_grad = cotangent.astype(jnp.float32) + inverse * (
            scaled_grad - normed * jnp.mean(scaled_grad * normed, axis=-1, keepdims=True)
        )
        input_grad = input_grad.astype(jnp.bfloat16)
        gain_term = gain_term + jnp.where(active_step, jnp.sum(normed_grad * normed, axis=0), 0.0)
        scaled_all = write_rows(scaled_all, scaled, first_row, active_step)
        cot_all = write_rows(cot_all, cotangent, first_row, active_step)
        pre_all = write_rows(pre_all, pre_grad, first_row, active_step)
        hidden_all = write_rows(hidden_all, hidden, first_row, active_step)
        grads_all = write_rows(grads_all, input_grad, first_row, active_step)
        outgoing = shifted(input_grad, "section", -1)
        return (outgoing, scaled_all, cot_all, pre_all, hidden_all, grads_all, gain_term)

    token_count = layer_inputs.shape[0]
    start_carry = (
        jnp.zeros((ROWS, width), jnp.bfloat16),
        jnp.zeros((token_count, width), jnp.bfloat16),
        jnp.zeros((token_count, width), jnp.bfloat16),
        jnp.zeros((token_count, rank_width), jnp.bfloat16),
        jnp.zeros((token_count, rank_width), jnp.bfloat16),
        jnp.zeros((token_count, width), jnp.bfloat16),
        jnp.zeros((width,), jnp.float32),
    )
    final_carry = lax.fori_loop(0, MICRO + sections - 1, run_step, start_carry)
    _, scaled_all, cot_all, pre_all, hidden_all, grads_all, gain_term = final_carry
    down_part = jnp.einsum("td,tr->dr", scaled_all, pre_all, preferred_element_type=jnp.float32)
    up_part = jnp.einsum("td,tr->dr", cot_all, hidden_all, preferred_element_type=jnp.float32)
    stacked = lax.psum_scatter(
        jnp.concatenate([down_part, up_part], axis=1).astype(jnp.bfloat16),
        "dp",
        scatter_dimension=0,
        tiled=True,
    ).astype(jnp.float32)
    gain_sum = lax.psum_scatter(gain_term, "dp", scatter_dimension=0, tiled=True)
    stacked = stacked / TOK_DEV
    grad_down = stacked[:, :rank_width]
    grad_up = stacked[:, rank_width:]
    return (grads_all[None], grad_down[None], grad_up[None], (gain_sum / TOK_DEV)[None])


def solution(mesh):
    in_specs = (
        P("section", "dp", None),
        P("dp", None),
        P("dp"),
        P("section", None),
        P("section", "dp", None),
        P("section", "dp", None),
    )
    out_specs = (
        P("section", "dp", None),
        P("section", "dp", None),
        P("section", "dp", None),
        P("section", "dp"),
    )
    return jax.shard_map(local, mesh=mesh, in_specs=in_specs, out_specs=out_specs, check_vma=False)
```

profile of v0, /device:TPU:0, one launch (start us, length us, event | category | flops | bytes accessed | tf_op | source)
XLA Modules:
  0.0 383.3 jit_solution(15505079731274536532)
XLA Ops:
  8.7 54.7 %all-gather.5.cloned.1.call-done = bf16[1,8192,256]{2,1,0:T(8,128)(2,1)} async-done(((bf16[1,512,256]{2,1,0:T(8,128)(2,1)}), bf16[1,8192,256]{2,1,0:T(8,128)(2,1)}) %all-gather.5.cloned.1.call-update) | async-done | bytes 4194320 | tf_op jit(solution)/shard_map/all_gather | solution.py:31
  63.5 51.2 %all-gather.7.cloned.1.call-done = bf16[1,8192,256]{2,1,0:T(8,128)(2,1)} async-done(((bf16[1,512,256]{2,1,0:T(8,128)(2,1)}), bf16[1,8192,256]{2,1,0:T(8,128)(2,1)}) %all-gather.7.cloned.1.call-update) | async-done | bytes 4194320 | tf_op jit(solution)/shard_map/all_gather | solution.py:32
  114.8 1.5 broadcast.67.clone.1
  116.3 1.5 broadcast.67.clone
  117.8 1.5 broadcast.67
  119.3 135.4 %while.28 = (s32[]{:T(128)}, bf16[32,8192]{1,0:T(8,128)(2,1)S(1)}, bf16[128,8192]{1,0:T(8,128)(2,1)}, bf16[128,8192]{1,0:T(8,128)(2,1)}, bf16[128,256]{1,0:T(8,1...) while((s32[]{:T(128)}, bf16[32,8192]{1,0:T(8,128)(2,1)S(1)}, ...), condition=%wide.region_4.5_spmd.clone, body=%wide.region_0.4_spmd.clone.sunk | while | flops 546234496 | bytes 63868848 | solution.py:91
  119.7 3.2 select_dynamic-update-slice_fusion.8
  123.1 2.4 fusion.48
  129.2 3.0 select_dynamic-update-slice_fusion.10
  133.5 14.7 %collective-permute-done = bf16[32,8192]{1,0:T(8,128)(2,1)S(1)} collective-permute-done((bf16[32,8192]{1,0:T(8,128)(2,1)S(1)}, bf16[32,8192]{1,0:T(8,128)(2,1)S(1)}, u32[]{:S(2)}, u32[]{:S(2)}) %collective-permute-start) | collective-permute-done | bytes 524320 | tf_op jit(solution)/shard_map/while/body/eval_jaxpr/ppermute | solution.py:15
  148.5 3.2 select_dynamic-update-slice_fusion.8
  152.0 2.4 fusion.48
  158.1 3.0 select_dynamic-update-slice_fusion.10
  162.4 13.8 %collective-permute-done = bf16[32,8192]{1,0:T(8,128)(2,1)S(1)} collective-permute-done((bf16[32,8192]{1,0:T(8,128)(2,1)S(1)}, bf16[32,8192]{1,0:T(8,128)(2,1)S(1)}, u32[]{:S(2)}, u32[]{:S(2)}) %collective-permute-start) | collective-permute-done | bytes 524320 | tf_op jit(solution)/shard_map/while/body/eval_jaxpr/ppermute | solution.py:15
  176.6 3.2 select_dynamic-update-slice_fusion.8
  180.0 2.4 fusion.48
  184.6 1.5 fusion.49
  186.1 3.0 select_dynamic-update-slice_fusion.10
  190.4 12.9 %collective-permute-done = bf16[32,8192]{1,0:T(8,128)(2,1)S(1)} collective-permute-done((bf16[32,8192]{1,0:T(8,128)(2,1)S(1)}, bf16[32,8192]{1,0:T(8,128)(2,1)S(1)}, u32[]{:S(2)}, u32[]{:S(2)}) %collective-permute-start) | collective-permute-done | bytes 524320 | tf_op jit(solution)/shard_map/while/body/eval_jaxpr/ppermute | solution.py:15
  203.7 3.2 select_dynamic-update-slice_fusion.8
  207.1 2.4 fusion.48
  213.2 3.0 select_dynamic-update-slice_fusion.10
  217.5 12.0 %collective-permute-done = bf16[32,8192]{1,0:T(8,128)(2,1)S(1)} collective-permute-done((bf16[32,8192]{1,0:T(8,128)(2,1)S(1)}, bf16[32,8192]{1,0:T(8,128)(2,1)S(1)}, u32[]{:S(2)}, u32[]{:S(2)}) %collective-permute-start) | collective-permute-done | bytes 524320 | tf_op jit(solution)/shard_map/while/body/eval_jaxpr/ppermute | solution.py:15
  229.8 3.2 select_dynamic-update-slice_fusion.8
  233.3 2.4 fusion.48
  239.3 3.0 select_dynamic-update-slice_fusion.10
  243.7 11.1 %collective-permute-done = bf16[32,8192]{1,0:T(8,128)(2,1)S(1)} collective-permute-done((bf16[32,8192]{1,0:T(8,128)(2,1)S(1)}, bf16[32,8192]{1,0:T(8,128)(2,1)S(1)}, u32[]{:S(2)}, u32[]{:S(2)}) %collective-permute-start) | collective-permute-done | bytes 524320 | tf_op jit(solution)/shard_map/while/body/eval_jaxpr/ppermute | solution.py:15
  254.8 5.0 %convolution_convert_fusion.1 = bf16[8192,256]{0,1:T(8,128)(2,1)} fusion(bf16[128,8192]{1,0:T(8,128)(2,1)} %get-tuple-element.369, bf16[128,256]{1,0:T(8,128)(2,1)S(1)} %get-tuple-element.370), kind=kOutput, calls=%fused_computation.36 | convolution fusion | flops 538968064 | bytes 6356992 | tf_op jit(solution)/shard_map/td,tr->dr/dot_general | solution.py:93
  259.7 3.2 convolution_convert_fusion
  263.0 7.7 %pad_maximum_fusion = bf16[8192,512]{0,1:T(8,128)(2,1)} fusion(bf16[8192,256]{0,1:T(8,128)(2,1)} %convolution_convert_fusion, bf16[8192,256]{0,1:T(8,128)(2,1)} %convolution_convert_fusion.1), kind=kLoop, calls=%fused_computation.37 | loop fusion | flops 16777216 | bytes 16777216 | tf_op jit(solution)/shard_map/concatenate | solution.py:96
  272.5 59.9 %all-reduce = f32[8192]{0:T(1024)S(1)} all-reduce(f32[8192]{0:T(1024)S(1)} %get-tuple-element.373), channel_id=5, replica_groups=mesh['section'=2,'dp'=16] {'dp'}, use_global_device_ids=true, to_apply=%region_6.7.clone | all-reduce | flops 8192 | bytes 65536
  333.1 40.4 %reduce-scatter.2.cloned.1.call-done = bf16[512,512]{0,1:T(8,128)(2,1)} async-done(((bf16[8192,512]{0,1:T(8,128)(2,1)}), bf16[512,512]{0,1:T(8,128)(2,1)}) %reduce-scatter.2.cloned.1.call-update) | async-done | bytes 524304 | tf_op jit(solution)/shard_map/reduce_scatter | solution.py:95
  (85 shorter events, 32.5 us)
Async XLA Ops:
  7.2 56.3 %all-gather.5.cloned.1.call-start = ((), (), s32[]{:S(2)}) async-start(), calls=%async_computation.2 | async-start | bytes 4456448 | tf_op jit(solution)/shard_map/all_gather | solution.py:31
  7.9 106.8 %all-gather.7.cloned.1.call-start = ((), (), s32[]{:S(2)}) async-start(), calls=%async_computation.3 | async-start | bytes 4456448 | tf_op jit(solution)/shard_map/all_gather | solution.py:32
  8.6 364.9 %reduce-scatter.2.cloned.1.call-start = ((), (), s32[]{:S(2)}) async-start(), calls=%async_computation.1 | async-start | bytes 8912896 | tf_op jit(solution)/shard_map/reduce_scatter | solution.py:95
  116.3 3.0 copy-start.2
  116.3 3.0 copy-start.4
  116.3 3.0 copy-start.5
  119.7 3.5 copy-start.1
  125.6 2.2 copy-start
  132.2 16.0 %collective-permute-start = (bf16[32,8192]{1,0:T(8,128)(2,1)S(1)}, bf16[32,8192]{1,0:T(8,128)(2,1)S(1)}, u32[]{:S(2)}, u32[]{:S(2)}) collective-permute-start(bf16[32,8192]{1,0:T(8,128)(2,1)S(1)} %get-tuple-element.590), channel_id=1, source_target_pairs={{16,0},{17,1},{18,2},{19,3},{20,4},{21,5},{22,6},{23,7},{24,8},{25... | collective-permute-start | bytes 1572872 | tf_op jit(solution)/shard_map/while/body/eval_jaxpr/ppermute | solution.py:15
  148.5 3.5 copy-start.1
  154.4 2.2 copy-start
  161.1 15.2 %collective-permute-start = (bf16[32,8192]{1,0:T(8,128)(2,1)S(1)}, bf16[32,8192]{1,0:T(8,128)(2,1)S(1)}, u32[]{:S(2)}, u32[]{:S(2)}) collective-permute-start(bf16[32,8192]{1,0:T(8,128)(2,1)S(1)} %get-tuple-element.590), channel_id=1, source_target_pairs={{16,0},{17,1},{18,2},{19,3},{20,4},{21,5},{22,6},{23,7},{24,8},{25... | collective-permute-start | bytes 1572872 | tf_op jit(solution)/shard_map/while/body/eval_jaxpr/ppermute | solution.py:15
  176.5 3.5 copy-start.1
  182.4 2.2 copy-start
  189.1 14.2 %collective-permute-start = (bf16[32,8192]{1,0:T(8,128)(2,1)S(1)}, bf16[32,8192]{1,0:T(8,128)(2,1)S(1)}, u32[]{:S(2)}, u32[]{:S(2)}) collective-permute-start(bf16[32,8192]{1,0:T(8,128)(2,1)S(1)} %get-tuple-element.590), channel_id=1, source_target_pairs={{16,0},{17,1},{18,2},{19,3},{20,4},{21,5},{22,6},{23,7},{24,8},{25... | collective-permute-start | bytes 1572872 | tf_op jit(solution)/shard_map/while/body/eval_jaxpr/ppermute | solution.py:15
  203.6 3.5 copy-start.1
  209.5 2.2 copy-start
  216.2 13.3 %collective-permute-start = (bf16[32,8192]{1,0:T(8,128)(2,1)S(1)}, bf16[32,8192]{1,0:T(8,128)(2,1)S(1)}, u32[]{:S(2)}, u32[]{:S(2)}) collective-permute-start(bf16[32,8192]{1,0:T(8,128)(2,1)S(1)} %get-tuple-element.590), channel_id=1, source_target_pairs={{16,0},{17,1},{18,2},{19,3},{20,4},{21,5},{22,6},{23,7},{24,8},{25... | collective-permute-start | bytes 1572872 | tf_op jit(solution)/shard_map/while/body/eval_jaxpr/ppermute | solution.py:15
  229.8 3.5 copy-start.1
  235.7 2.2 copy-start
  242.4 12.4 %collective-permute-start = (bf16[32,8192]{1,0:T(8,128)(2,1)S(1)}, bf16[32,8192]{1,0:T(8,128)(2,1)S(1)}, u32[]{:S(2)}, u32[]{:S(2)}) collective-permute-start(bf16[32,8192]{1,0:T(8,128)(2,1)S(1)} %get-tuple-element.590), channel_id=1, source_target_pairs={{16,0},{17,1},{18,2},{19,3},{20,4},{21,5},{22,6},{23,7},{24,8},{25... | collective-permute-start | bytes 1572872 | tf_op jit(solution)/shard_map/while/body/eval_jaxpr/ppermute | solution.py:15
  254.8 5.0 %copy-start.3 = (bf16[128,8192]{1,0:T(8,128)(2,1)S(1)}, bf16[128,8192]{1,0:T(8,128)(2,1)}, u32[]{:S(2)}) copy-start(bf16[128,8192]{1,0:T(8,128)(2,1)} %get-tuple-element.371) | copy-start | bytes 6291460
  270.7 0.7 copy-start.6
Sparse Core Ops, SparseCore 0:
  10.2 53.2 all-gather.4
  65.6 49.0 all-gather.6
  270.8 102.6 reduce-scatter.1
where the time goes:
time: 384 us; the launch traced here: 383 us
  waiting for transfers between devices  212 us (55%)
  blocking collectives  59.9 us (16%)
  matrix products  47.9 us (12%)
  other arithmetic  26.3 us (7%)
  local copies, waits for them, and re-layouts  15.7 us (4%)
  between operations  14.5 us (4%)
  starting transfers between devices  6.52 us (2%)
    ppermute x5, waiting for transfers between devices, shifted(): return lax.ppermute(block, axis, route)  64.5 us
    unnamed x1, blocking collectives  59.9 us
    all_gather x1, waiting for transfers between devices, local(): lax.all_gather(w_down[0], 'dp', axis=0, tiled=True)  54.7 us
    all_gather x1, waiting for transfers between devices, local(): lax.all_gather(w_up[0], 'dp', axis=0, tiled=True)  51.2 us
    reduce_scatter x1, waiting for transfers between devices, local(): lax.psum_scatter(jnp.concatenate([down_part, up_part], axis=1).astype(jnp...  40.4 us
    dot_general x5, matrix products, run_step(): preact = jnp.dot(scaled, down_matrix, preferred_element_type=jnp.float32)  16.2 us
    dynamic_update_slice x5, other arithmetic, write_rows(): lax.dynamic_update_slice_in_dim(buffer, jnp.where(active_step, fresh, pre...  15.1 us
    dot_general x5, matrix products, run_step(): jnp.einsum('tr,dr->td', hidden, up_matrix, preferred_element_type=jnp.flo...  12 us
  transfers between devices with their start and end apart: 8, of which 8 were waited for; matrix products, arithmetic and copies ran while one was open for 0% of the time, Pallas kernels for 0%

commit v1 on v0

--- a/solution.py
+++ b/solution.py
@@ -7,6 +7,28 @@
 ROWS = 32
 TOK_DEV = 128
 EPSILON = 1e-05
+
+
+def laid_out(tiles, dim):
+    lengths = list(tiles.shape[1:])
+    lengths[dim] *= tiles.shape[0]
+    return jnp.moveaxis(tiles, 0, dim).reshape(lengths)
+
+
+def ring_gather(x, axis, dim):
+    devices = lax.axis_size(axis)
+    pairs = [(i, (i + 1) % devices) for i in range(devices)]
+    back = [(b, a) for a, b in pairs]
+    lower, upper = ([], [])
+    for step in range(devices - 1):
+        if step % 2 == 0:
+            lower.append(lax.ppermute(lower[-1] if lower else x, axis, pairs))
+        else:
+            upper.append(lax.ppermute(upper[-1] if upper else x, axis, back))
+    parts = jnp.stack([*lower[::-1], x, *upper])
+    shift = lax.axis_index(axis) - len(lower)
+    parts = parts[(jnp.arange(devices) - shift) % devices]
+    return laid_out(parts, dim)
 
 
 def shifted(block, axis, distance):
@@ -28,7 +50,7 @@
     layer_inputs = section_inputs[0]
     gain = gains[0]
     down_matrix, up_matrix = (
-        lax.all_gather(w_down[0], "dp", axis=0, tiled=True),
+        ring_gather(w_down[0], "dp", 0),
         lax.all_gather(w_up[0], "dp", axis=0, tiled=True),
     )
     is_last = section_index == sections - 1

time: 384 us -> 370 us (0.964)
  waiting for transfers between devices: 212 us -> 140 us
  starting transfers between devices: 6.52 us -> 39.3 us
  blocking collectives: 59.9 us -> 72.4 us
  local copies, waits for them, and re-layouts: 15.7 us -> 27.4 us
    all_gather x1 -> x0, waiting for transfers between devices: 54.7 us -> none  [local(): lax.all_gather(w_down[0], 'dp', axis=0, tiled=True)]
    all_gather x1, waiting for transfers between devices: 51.2 us -> 0.01 us  [local(): lax.all_gather(w_up[0], 'dp', axis=0, tiled=True)]
    ppermute x0 -> x15, waiting for transfers between devices: none -> 46.3 us  [the longest x8 28.4 us: ring_gather(): lower.append(lax.ppermute(lower[-1] if lower else x, axis, pairs))]
    ppermute x0 -> x15, starting transfers between devices: none -> 32.8 us  [the longest x7 32.3 us: ring_gather(): upper.append(lax.ppermute(upper[-1] if upper else x, axis, back))]
    ppermute x5, waiting for transfers between devices: 64.5 us -> 48.8 us  [shifted(): return lax.ppermute(block, axis, route)]
    unnamed x13 -> x30, local copies, waits for them, and re-layouts: 3.21 us -> 15.9 us
    unnamed x1, blocking collectives: 59.9 us -> 72.4 us
    while x20, local copies, waits for them, and re-layouts: 7.77 us -> 1.11 us
  transfers between devices with their start and end apart: 8 -> 22, of which waited for: 8 -> 20; matrix products, arithmetic and copies ran while one was open for 0% -> 5% of each run, Pallas kernels for 0% -> 0%
where the time goes in v1:
time: 370 us
  waiting for transfers between devices  140 us (38%)
  blocking collectives  72.4 us (20%)
  matrix products  48.6 us (13%)
  starting transfers between devices  39.3 us (11%)
  local copies, waits for them, and re-layouts  27.4 us (7%)
  other arithmetic  26.3 us (7%)
  between operations  14.8 us (4%)
    unnamed x1, blocking collectives  72.4 us
    ppermute x5, waiting for transfers between devices, shifted(): return lax.ppermute(block, axis, route)  48.8 us
    reduce_scatter x1, waiting for transfers between devices, local(): lax.psum_scatter(jnp.concatenate([down_part, up_part], axis=1).astype(jnp...  44.7 us
    ppermute x7, starting transfers between devices, ring_gather(): upper.append(lax.ppermute(upper[-1] if upper else x, axis, back))  32.3 us
    ppermute x8, waiting for transfers between devices, ring_gather(): lower.append(lax.ppermute(lower[-1] if lower else x, axis, pairs))  28.4 us
    ppermute x7, waiting for transfers between devices, ring_gather(): upper.append(lax.ppermute(upper[-1] if upper else x, axis, back))  17.9 us
    dot_general x5, matrix products, run_step(): preact = jnp.dot(scaled, down_matrix, preferred_element_type=jnp.float32)  16.1 us
    unnamed x30, local copies, waits for them, and re-layouts  15.9 us
  transfers between devices with their start and end apart: 22, of which 20 were waited for; matrix products, arithmetic and copies ran while one was open for 5% of the time, Pallas kernels for 0%

profile of v1, /device:TPU:0, one launch (start us, length us, event | category | flops | bytes accessed | tf_op | source)
XLA Modules:
  0.0 369.7 jit_solution(1765230415330807652)
XLA Ops:
  8.5 9.3 %collective-permute-done.1 = bf16[512,256]{1,0:T(8,128)(2,1)S(1)} collective-permute-done((bf16[512,256]{1,0:T(8,128)(2,1)}, bf16[512,256]{1,0:T(8,128)(2,1)S(1)}, u32[]{:S(2)}, u32[]{:S(2)}) %collective-permute-start.1) | collective-permute-done | bytes 262176 | tf_op jit(solution)/shard_map/ppermute | solution.py:25
  17.7 4.4 %collective-permute-start.9 = (bf16[512,256]{1,0:T(8,128)(2,1)}, bf16[512,256]{1,0:T(8,128)(2,1)S(1)}, u32[]{:S(2)}, u32[]{:S(2)}) collective-permute-start(bf16[512,256]{1,0:T(8,128)(2,1)} %bitcast.76), channel_id=1, source_target_pairs={{1,0},{2,1},{3,2},{4,3},{5,4},{6,5},{7,6},{8,7},{9,8},{10,9},{11,1... | collective-permute-start | bytes 786440 | tf_op jit(solution)/shard_map/ppermute | solution.py:27
  22.2 4.3 %collective-permute-done.2 = bf16[512,256]{1,0:T(8,128)(2,1)S(1)} collective-permute-done((bf16[512,256]{1,0:T(8,128)(2,1)S(1)}, bf16[512,256]{1,0:T(8,128)(2,1)S(1)}, u32[]{:S(2)}, u32[]{:S(2)}) %collective-permute-start.2) | collective-permute-done | bytes 262176 | tf_op jit(solution)/shard_map/ppermute | solution.py:25
  27.3 4.6 %collective-permute-start.10 = (bf16[512,256]{1,0:T(8,128)(2,1)S(1)}, bf16[512,256]{1,0:T(8,128)(2,1)S(1)}, u32[]{:S(2)}, u32[]{:S(2)}) collective-permute-start(bf16[512,256]{1,0:T(8,128)(2,1)S(1)} %collective-permute-done.9), channel_id=1, source_target_pairs={{1,0},{2,1},{3,2},{4,3},{5,4},{6,5},{7,6},{8,7},{9,8},{10,9},{11,1... | collective-permute-start | bytes 786440 | tf_op jit(solution)/shard_map/ppermute | solution.py:27
  31.9 4.5 %collective-permute-done.3 = bf16[512,256]{1,0:T(8,128)(2,1)S(1)} collective-permute-done((bf16[512,256]{1,0:T(8,128)(2,1)S(1)}, bf16[512,256]{1,0:T(8,128)(2,1)S(1)}, u32[]{:S(2)}, u32[]{:S(2)}) %collective-permute-start.3) | collective-permute-done | bytes 262176 | tf_op jit(solution)/shard_map/ppermute | solution.py:25
  37.5 4.7 %collective-permute-start.11 = (bf16[512,256]{1,0:T(8,128)(2,1)S(1)}, bf16[512,256]{1,0:T(8,128)(2,1)S(1)}, u32[]{:S(2)}, u32[]{:S(2)}) collective-permute-start(bf16[512,256]{1,0:T(8,128)(2,1)S(1)} %collective-permute-done.10), channel_id=1, source_target_pairs={{1,0},{2,1},{3,2},{4,3},{5,4},{6,5},{7,6},{8,7},{9,8},{10,9},{11,1... | collective-permute-start | bytes 786440 | tf_op jit(solution)/shard_map/ppermute | solution.py:27
  44.9 6.1 %collective-permute-done.11 = bf16[512,256]{1,0:T(8,128)(2,1)S(1)} collective-permute-done((bf16[512,256]{1,0:T(8,128)(2,1)S(1)}, bf16[512,256]{1,0:T(8,128)(2,1)S(1)}, u32[]{:S(2)}, u32[]{:S(2)}) %collective-permute-start.11) | collective-permute-done | bytes 262176 | tf_op jit(solution)/shard_map/ppermute | solution.py:27
  51.0 4.6 %collective-permute-start.12 = (bf16[512,256]{1,0:T(8,128)(2,1)S(1)}, bf16[512,256]{1,0:T(8,128)(2,1)S(1)}, u32[]{:S(2)}, u32[]{:S(2)}) collective-permute-start(bf16[512,256]{1,0:T(8,128)(2,1)S(1)} %collective-permute-done.11), channel_id=1, source_target_pairs={{1,0},{2,1},{3,2},{4,3},{5,4},{6,5},{7,6},{8,7},{9,8},{10,9},{11,1... | collective-permute-start | bytes 786440 | tf_op jit(solution)/shard_map/ppermute | solution.py:27
  55.6 3.4 collective-permute-done.5
  59.7 4.7 %collective-permute-start.13 = (bf16[512,256]{1,0:T(8,128)(2,1)S(1)}, bf16[512,256]{1,0:T(8,128)(2,1)S(1)}, u32[]{:S(2)}, u32[]{:S(2)}) collective-permute-start(bf16[512,256]{1,0:T(8,128)(2,1)S(1)} %collective-permute-done.12), channel_id=1, source_target_pairs={{1,0},{2,1},{3,2},{4,3},{5,4},{6,5},{7,6},{8,7},{9,8},{10,9},{11,1... | collective-permute-start | bytes 786440 | tf_op jit(solution)/shard_map/ppermute | solution.py:27
  64.4 3.3 collective-permute-done.6
  67.6 5.6 %collective-permute-done.13 = bf16[512,256]{1,0:T(8,128)(2,1)S(1)} collective-permute-done((bf16[512,256]{1,0:T(8,128)(2,1)S(1)}, bf16[512,256]{1,0:T(8,128)(2,1)S(1)}, u32[]{:S(2)}, u32[]{:S(2)}) %collective-permute-start.13) | collective-permute-done | bytes 262176 | tf_op jit(solution)/shard_map/ppermute | solution.py:27
  73.3 4.6 %collective-permute-start.14 = (bf16[512,256]{1,0:T(8,128)(2,1)S(1)}, bf16[512,256]{1,0:T(8,128)(2,1)S(1)}, u32[]{:S(2)}, u32[]{:S(2)}) collective-permute-start(bf16[512,256]{1,0:T(8,128)(2,1)S(1)} %collective-permute-done.13), channel_id=1, source_target_pairs={{1,0},{2,1},{3,2},{4,3},{5,4},{6,5},{7,6},{8,7},{9,8},{10,9},{11,1... | collective-permute-start | bytes 786440 | tf_op jit(solution)/shard_map/ppermute | solution.py:27
  78.4 3.4 collective-permute-done.14
  81.8 4.7 %collective-permute-start.15 = (bf16[512,256]{1,0:T(8,128)(2,1)S(1)}, bf16[512,256]{1,0:T(8,128)(2,1)S(1)}, u32[]{:S(2)}, u32[]{:S(2)}) collective-permute-start(bf16[512,256]{1,0:T(8,128)(2,1)S(1)} %collective-permute-done.14), channel_id=1, source_target_pairs={{1,0},{2,1},{3,2},{4,3},{5,4},{6,5},{7,6},{8,7},{9,8},{10,9},{11,1... | collective-permute-start | bytes 786440 | tf_op jit(solution)/shard_map/ppermute | solution.py:27
  100.5 5.0 %gather_fusion = bf16[16,512,256]{2,1,0:T(8,128)(2,1)} fusion(bf16[16,512,256]{2,1,0:T(8,128)(2,1)} %bitcast_dynamic-update-slice_fusion, s32[1024]{0:T(1024)S(1)} %pad_clamp_fusion), kind=kCustom, calls=%fused_computation | custom fusion | bytes 8388672 | tf_op jit(solution)/shard_map/gather | solution.py:30
  110.3 113.8 %while.28 = (s32[]{:T(128)}, bf16[32,8192]{1,0:T(8,128)(2,1)S(1)}, bf16[128,8192]{1,0:T(8,128)(2,1)}, bf16[128,8192]{1,0:T(8,128)(2,1)}, bf16[128,256]{1,0:T(8,1...) while((s32[]{:T(128)}, bf16[32,8192]{1,0:T(8,128)(2,1)S(1)}, ...), condition=%wide.region_4.5_spmd.clone, body=%wide.region_0.4_spmd.clone.sunk | while | flops 546234496 | bytes 63868848 | solution.py:113
  110.6 3.2 select_dynamic-update-slice_fusion.8
  123.3 9.8 %collective-permute-done = bf16[32,8192]{1,0:T(8,128)(2,1)S(1)} collective-permute-done((bf16[32,8192]{1,0:T(8,128)(2,1)S(1)}, bf16[32,8192]{1,0:T(8,128)(2,1)S(1)}, u32[]{:S(2)}, u32[]{:S(2)}) %collective-permute-start) | collective-permute-done | bytes 524320 | tf_op jit(solution)/shard_map/while/body/eval_jaxpr/ppermute | solution.py:37
  133.4 3.2 select_dynamic-update-slice_fusion.8
  146.0 9.8 %collective-permute-done = bf16[32,8192]{1,0:T(8,128)(2,1)S(1)} collective-permute-done((bf16[32,8192]{1,0:T(8,128)(2,1)S(1)}, bf16[32,8192]{1,0:T(8,128)(2,1)S(1)}, u32[]{:S(2)}, u32[]{:S(2)}) %collective-permute-start) | collective-permute-done | bytes 524320 | tf_op jit(solution)/shard_map/while/body/eval_jaxpr/ppermute | solution.py:37
  156.1 3.2 select_dynamic-update-slice_fusion.8
  168.8 9.8 %collective-permute-done = bf16[32,8192]{1,0:T(8,128)(2,1)S(1)} collective-permute-done((bf16[32,8192]{1,0:T(8,128)(2,1)S(1)}, bf16[32,8192]{1,0:T(8,128)(2,1)S(1)}, u32[]{:S(2)}, u32[]{:S(2)}) %collective-permute-start) | collective-permute-done | bytes 524320 | tf_op jit(solution)/shard_map/while/body/eval_jaxpr/ppermute | solution.py:37
  178.9 3.2 select_dynamic-update-slice_fusion.8
  191.5 9.8 %collective-permute-done = bf16[32,8192]{1,0:T(8,128)(2,1)S(1)} collective-permute-done((bf16[32,8192]{1,0:T(8,128)(2,1)S(1)}, bf16[32,8192]{1,0:T(8,128)(2,1)S(1)}, u32[]{:S(2)}, u32[]{:S(2)}) %collective-permute-start) | collective-permute-done | bytes 524320 | tf_op jit(solution)/shard_map/while/body/eval_jaxpr/ppermute | solution.py:37
  201.6 3.2 select_dynamic-update-slice_fusion.8
  214.3 9.8 %collective-permute-done = bf16[32,8192]{1,0:T(8,128)(2,1)S(1)} collective-permute-done((bf16[32,8192]{1,0:T(8,128)(2,1)S(1)}, bf16[32,8192]{1,0:T(8,128)(2,1)S(1)}, u32[]{:S(2)}, u32[]{:S(2)}) %collective-permute-start) | collective-permute-done | bytes 524320 | tf_op jit(solution)/shard_map/while/body/eval_jaxpr/ppermute | solution.py:37
  224.0 5.0 %convolution_convert_fusion.1 = bf16[8192,256]{0,1:T(8,128)(2,1)} fusion(bf16[128,8192]{1,0:T(8,128)(2,1)} %get-tuple-element.369, bf16[128,256]{1,0:T(8,128)(2,1)S(1)} %get-tuple-element.370), kind=kOutput, calls=%fused_computation.37 | convolution fusion | flops 538968064 | bytes 6356992 | tf_op jit(solution)/shard_map/td,tr->dr/dot_general | solution.py:115
  229.0 3.2 convolution_convert_fusion
  232.3 7.7 %pad_maximum_fusion = bf16[8192,512]{0,1:T(8,128)(2,1)} fusion(bf16[8192,256]{0,1:T(8,128)(2,1)} %convolution_convert_fusion, bf16[8192,256]{0,1:T(8,128)(2,1)} %convolution_convert_fusion.1), kind=kLoop, calls=%fused_computation.38 | loop fusion | flops 16777216 | bytes 16777216 | tf_op jit(solution)/shard_map/concatenate | solution.py:118
  241.9 72.4 %all-reduce = f32[8192]{0:T(1024)S(1)} all-reduce(f32[8192]{0:T(1024)S(1)} %get-tuple-element.373), channel_id=4, replica_groups=mesh['section'=2,'dp'=16] {'dp'}, use_global_device_ids=true, to_apply=%region_6.7.clone | all-reduce | flops 8192 | bytes 65536
  314.9 44.7 %reduce-scatter.2.cloned.1.call-done = bf16[512,512]{0,1:T(8,128)(2,1)} async-done(((bf16[8192,512]{0,1:T(8,128)(2,1)}), bf16[512,512]{0,1:T(8,128)(2,1)}) %reduce-scatter.2.cloned.1.call-update) | async-done | bytes 524304 | tf_op jit(solution)/shard_map/reduce_scatter | solution.py:117
  (133 shorter events, 79.6 us)
Async XLA Ops:
  7.2 87.6 %copy-start.5 = (bf16[1,512,256]{2,1,0:T(8,128)(2,1)S(1)}, bf16[1,512,256]{2,1,0:T(8,128)(2,1)}, u32[]{:S(2)}) copy-start(bf16[1,512,256]{2,1,0:T(8,128)(2,1)} %param.12) | copy-start | bytes 786436
  7.2 98.4 %all-gather.3.cloned.1.call-start = ((), (), s32[]{:S(2)}) async-start(), calls=%async_computation.2 | async-start | bytes 4456448 | tf_op jit(solution)/shard_map/all_gather | solution.py:54
  7.9 351.7 %reduce-scatter.2.cloned.1.call-start = ((), (), s32[]{:S(2)}) async-start(), calls=%async_computation.1 | async-start | bytes 8912896 | tf_op jit(solution)/shard_map/reduce_scatter | solution.py:117
  8.0 9.8 %collective-permute-start.1 = (bf16[512,256]{1,0:T(8,128)(2,1)}, bf16[512,256]{1,0:T(8,128)(2,1)S(1)}, u32[]{:S(2)}, u32[]{:S(2)}) collective-permute-start(bf16[512,256]{1,0:T(8,128)(2,1)} %bitcast.75), channel_id=1, source_target_pairs={{0,1},{1,2},{2,3},{3,4},{4,5},{5,6},{6,7},{7,8},{8,9},{9,10},{10,1... | collective-permute-start | bytes 786440 | tf_op jit(solution)/shard_map/ppermute | solution.py:25
  17.7 8.7 %collective-permute-start.2 = (bf16[512,256]{1,0:T(8,128)(2,1)S(1)}, bf16[512,256]{1,0:T(8,128)(2,1)S(1)}, u32[]{:S(2)}, u32[]{:S(2)}) collective-permute-start(bf16[512,256]{1,0:T(8,128)(2,1)S(1)} %collective-permute-done.1), channel_id=1, source_target_pairs={{0,1},{1,2},{2,3},{3,4},{4,5},{5,6},{6,7},{7,8},{8,9},{9,10},{10,1... | collective-permute-start | bytes 786440 | tf_op jit(solution)/shard_map/ppermute | solution.py:25
  17.7 9.5 %collective-permute-start.9 = (bf16[512,256]{1,0:T(8,128)(2,1)}, bf16[512,256]{1,0:T(8,128)(2,1)S(1)}, u32[]{:S(2)}, u32[]{:S(2)}) collective-permute-start(bf16[512,256]{1,0:T(8,128)(2,1)} %bitcast.76), channel_id=1, source_target_pairs={{1,0},{2,1},{3,2},{4,3},{5,4},{6,5},{7,6},{8,7},{9,8},{10,9},{11,1... | collective-permute-start | bytes 786440 | tf_op jit(solution)/shard_map/ppermute | solution.py:27
  26.4 9.9 %collective-permute-start.3 = (bf16[512,256]{1,0:T(8,128)(2,1)S(1)}, bf16[512,256]{1,0:T(8,128)(2,1)S(1)}, u32[]{:S(2)}, u32[]{:S(2)}) collective-permute-start(bf16[512,256]{1,0:T(8,128)(2,1)S(1)} %collective-permute-done.2), channel_id=1, source_target_pairs={{0,1},{1,2},{2,3},{3,4},{4,5},{5,6},{6,7},{7,8},{8,9},{9,10},{10,1... | collective-permute-start | bytes 786440 | tf_op jit(solution)/shard_map/ppermute | solution.py:25
  27.3 10.3 %collective-permute-start.10 = (bf16[512,256]{1,0:T(8,128)(2,1)S(1)}, bf16[512,256]{1,0:T(8,128)(2,1)S(1)}, u32[]{:S(2)}, u32[]{:S(2)}) collective-permute-start(bf16[512,256]{1,0:T(8,128)(2,1)S(1)} %collective-permute-done.9), channel_id=1, source_target_pairs={{1,0},{2,1},{3,2},{4,3},{5,4},{6,5},{7,6},{8,7},{9,8},{10,9},{11,1... | collective-permute-start | bytes 786440 | tf_op jit(solution)/shard_map/ppermute | solution.py:27
  36.3 8.6 %collective-permute-start.4 = (bf16[512,256]{1,0:T(8,128)(2,1)S(1)}, bf16[512,256]{1,0:T(8,128)(2,1)S(1)}, u32[]{:S(2)}, u32[]{:S(2)}) collective-permute-start(bf16[512,256]{1,0:T(8,128)(2,1)S(1)} %collective-permute-done.3), channel_id=1, source_target_pairs={{0,1},{1,2},{2,3},{3,4},{4,5},{5,6},{6,7},{7,8},{8,9},{9,10},{10,1... | collective-permute-start | bytes 786440 | tf_op jit(solution)/shard_map/ppermute | solution.py:25
  37.5 13.4 %collective-permute-start.11 = (bf16[512,256]{1,0:T(8,128)(2,1)S(1)}, bf16[512,256]{1,0:T(8,128)(2,1)S(1)}, u32[]{:S(2)}, u32[]{:S(2)}) collective-permute-start(bf16[512,256]{1,0:T(8,128)(2,1)S(1)} %collective-permute-done.10), channel_id=1, source_target_pairs={{1,0},{2,1},{3,2},{4,3},{5,4},{6,5},{7,6},{8,7},{9,8},{10,9},{11,1... | collective-permute-start | bytes 786440 | tf_op jit(solution)/shard_map/ppermute | solution.py:27
  44.9 14.1 %collective-permute-start.5 = (bf16[512,256]{1,0:T(8,128)(2,1)S(1)}, bf16[512,256]{1,0:T(8,128)(2,1)S(1)}, u32[]{:S(2)}, u32[]{:S(2)}) collective-permute-start(bf16[512,256]{1,0:T(8,128)(2,1)S(1)} %collective-permute-done.4), channel_id=1, source_target_pairs={{0,1},{1,2},{2,3},{3,4},{4,5},{5,6},{6,7},{7,8},{8,9},{9,10},{10,1... | collective-permute-start | bytes 786440 | tf_op jit(solution)/shard_map/ppermute | solution.py:25
  51.0 8.7 %collective-permute-start.12 = (bf16[512,256]{1,0:T(8,128)(2,1)S(1)}, bf16[512,256]{1,0:T(8,128)(2,1)S(1)}, u32[]{:S(2)}, u32[]{:S(2)}) collective-permute-start(bf16[512,256]{1,0:T(8,128)(2,1)S(1)} %collective-permute-done.11), channel_id=1, source_target_pairs={{1,0},{2,1},{3,2},{4,3},{5,4},{6,5},{7,6},{8,7},{9,8},{10,9},{11,1... | collective-permute-start | bytes 786440 | tf_op jit(solution)/shard_map/ppermute | solution.py:27
  59.0 8.6 %collective-permute-start.6 = (bf16[512,256]{1,0:T(8,128)(2,1)S(1)}, bf16[512,256]{1,0:T(8,128)(2,1)S(1)}, u32[]{:S(2)}, u32[]{:S(2)}) collective-permute-start(bf16[512,256]{1,0:T(8,128)(2,1)S(1)} %collective-permute-done.5), channel_id=1, source_target_pairs={{0,1},{1,2},{2,3},{3,4},{4,5},{5,6},{6,7},{7,8},{8,9},{9,10},{10,1... | collective-permute-start | bytes 786440 | tf_op jit(solution)/shard_map/ppermute | solution.py:25
  59.7 13.6 %collective-permute-start.13 = (bf16[512,256]{1,0:T(8,128)(2,1)S(1)}, bf16[512,256]{1,0:T(8,128)(2,1)S(1)}, u32[]{:S(2)}, u32[]{:S(2)}) collective-permute-start(bf16[512,256]{1,0:T(8,128)(2,1)S(1)} %collective-permute-done.12), channel_id=1, source_target_pairs={{1,0},{2,1},{3,2},{4,3},{5,4},{6,5},{7,6},{8,7},{9,8},{10,9},{11,1... | collective-permute-start | bytes 786440 | tf_op jit(solution)/shard_map/ppermute | solution.py:27
  67.6 10.7 %collective-permute-start.7 = (bf16[512,256]{1,0:T(8,128)(2,1)S(1)}, bf16[512,256]{1,0:T(8,128)(2,1)}, u32[]{:S(2)}, u32[]{:S(2)}) collective-permute-start(bf16[512,256]{1,0:T(8,128)(2,1)S(1)} %collective-permute-done.6), channel_id=1, source_target_pairs={{0,1},{1,2},{2,3},{3,4},{4,5},{5,6},{6,7},{7,8},{8,9},{9,10},{10,1... | collective-permute-start | bytes 786440 | tf_op jit(solution)/shard_map/ppermute | solution.py:25
  73.3 8.5 %collective-permute-start.14 = (bf16[512,256]{1,0:T(8,128)(2,1)S(1)}, bf16[512,256]{1,0:T(8,128)(2,1)S(1)}, u32[]{:S(2)}, u32[]{:S(2)}) collective-permute-start(bf16[512,256]{1,0:T(8,128)(2,1)S(1)} %collective-permute-done.13), channel_id=1, source_target_pairs={{1,0},{2,1},{3,2},{4,3},{5,4},{6,5},{7,6},{8,7},{9,8},{10,9},{11,1... | collective-permute-start | bytes 786440 | tf_op jit(solution)/shard_map/ppermute | solution.py:27
  78.3 8.8 %collective-permute-start.8 = (bf16[512,256]{1,0:T(8,128)(2,1)}, bf16[512,256]{1,0:T(8,128)(2,1)}, u32[]{:S(2)}, u32[]{:S(2)}) collective-permute-start(bf16[512,256]{1,0:T(8,128)(2,1)} %collective-permute-done.7), channel_id=1, source_target_pairs={{0,1},{1,2},{2,3},{3,4},{4,5},{5,6},{6,7},{7,8},{8,9},{9,10},{10,1... | collective-permute-start | bytes 786440 | tf_op jit(solution)/shard_map/ppermute | solution.py:25
  81.8 18.0 %collective-permute-start.15 = (bf16[512,256]{1,0:T(8,128)(2,1)S(1)}, bf16[512,256]{1,0:T(8,128)(2,1)S(1)}, u32[]{:S(2)}, u32[]{:S(2)}) collective-permute-start(bf16[512,256]{1,0:T(8,128)(2,1)S(1)} %collective-permute-done.14), channel_id=1, source_target_pairs={{1,0},{2,1},{3,2},{4,3},{5,4},{6,5},{7,6},{8,7},{9,8},{10,9},{11,1... | collective-permute-start | bytes 786440 | tf_op jit(solution)/shard_map/ppermute | solution.py:27
  105.5 4.7 %copy-start.2 = (bf16[1,128,8192]{2,1,0:T(8,128)(2,1)S(1)}, bf16[1,128,8192]{2,1,0:T(8,128)(2,1)}, u32[]{:S(2)}) copy-start(bf16[1,128,8192]{2,1,0:T(8,128)(2,1)} %param.8) | copy-start | bytes 6291460
  105.5 4.7 %copy-start.4 = (f32[1,8192]{1,0:T(1,128)S(1)}, f32[1,8192]{1,0:T(1,128)}, u32[]{:S(2)}) copy-start(f32[1,8192]{1,0:T(1,128)} %param.11) | copy-start | bytes 98308
  105.5 4.7 %copy-start.6 = (s32[128]{0:T(128)S(1)}, s32[128]{0:T(128)}, u32[]{:S(2)}) copy-start(s32[128]{0:T(128)} %param.10) | copy-start | bytes 1540
  110.6 3.4 copy-start.1
  122.0 11.1 %collective-permute-start = (bf16[32,8192]{1,0:T(8,128)(2,1)S(1)}, bf16[32,8192]{1,0:T(8,128)(2,1)S(1)}, u32[]{:S(2)}, u32[]{:S(2)}) collective-permute-start(bf16[32,8192]{1,0:T(8,128)(2,1)S(1)} %get-tuple-element.590), channel_id=1, source_target_pairs={{16,0},{17,1},{18,2},{19,3},{20,4},{21,5},{22,6},{23,7},{24,8},{25... | collective-permute-start | bytes 1572872 | tf_op jit(solution)/shard_map/while/body/eval_jaxpr/ppermute | solution.py:37
  133.4 3.4 copy-start.1
  144.7 11.1 %collective-permute-start = (bf16[32,8192]{1,0:T(8,128)(2,1)S(1)}, bf16[32,8192]{1,0:T(8,128)(2,1)S(1)}, u32[]{:S(2)}, u32[]{:S(2)}) collective-permute-start(bf16[32,8192]{1,0:T(8,128)(2,1)S(1)} %get-tuple-element.590), channel_id=1, source_target_pairs={{16,0},{17,1},{18,2},{19,3},{20,4},{21,5},{22,6},{23,7},{24,8},{25... | collective-permute-start | bytes 1572872 | tf_op jit(solution)/shard_map/while/body/eval_jaxpr/ppermute | solution.py:37
  156.1 3.4 copy-start.1
  167.5 11.1 %collective-permute-start = (bf16[32,8192]{1,0:T(8,128)(2,1)S(1)}, bf16[32,8192]{1,0:T(8,128)(2,1)S(1)}, u32[]{:S(2)}, u32[]{:S(2)}) collective-permute-start(bf16[32,8192]{1,0:T(8,128)(2,1)S(1)} %get-tuple-element.590), channel_id=1, source_target_pairs={{16,0},{17,1},{18,2},{19,3},{20,4},{21,5},{22,6},{23,7},{24,8},{25... | collective-permute-start | bytes 1572872 | tf_op jit(solution)/shard_map/while/body/eval_jaxpr/ppermute | solution.py:37
  178.9 3.4 copy-start.1
  190.2 11.1 %collective-permute-start = (bf16[32,8192]{1,0:T(8,128)(2,1)S(1)}, bf16[32,8192]{1,0:T(8,128)(2,1)S(1)}, u32[]{:S(2)}, u32[]{:S(2)}) collective-permute-start(bf16[32,8192]{1,0:T(8,128)(2,1)S(1)} %get-tuple-element.590), channel_id=1, source_target_pairs={{16,0},{17,1},{18,2},{19,3},{20,4},{21,5},{22,6},{23,7},{24,8},{25... | collective-permute-start | bytes 1572872 | tf_op jit(solution)/shard_map/while/body/eval_jaxpr/ppermute | solution.py:37
  201.6 3.4 copy-start.1
  213.0 11.1 %collective-permute-start = (bf16[32,8192]{1,0:T(8,128)(2,1)S(1)}, bf16[32,8192]{1,0:T(8,128)(2,1)S(1)}, u32[]{:S(2)}, u32[]{:S(2)}) collective-permute-start(bf16[32,8192]{1,0:T(8,128)(2,1)S(1)} %get-tuple-element.590), channel_id=1, source_target_pairs={{16,0},{17,1},{18,2},{19,3},{20,4},{21,5},{22,6},{23,7},{24,8},{25... | collective-permute-start | bytes 1572872 | tf_op jit(solution)/shard_map/while/body/eval_jaxpr/ppermute | solution.py:37
  224.0 5.0 %copy-start.3 = (bf16[128,8192]{1,0:T(8,128)(2,1)S(1)}, bf16[128,8192]{1,0:T(8,128)(2,1)}, u32[]{:S(2)}) copy-start(bf16[128,8192]{1,0:T(8,128)(2,1)} %get-tuple-element.371) | copy-start | bytes 6291460
  (6 other events, 17.7 us)
Sparse Core Ops, SparseCore 0:
  10.2 66.4 all-gather.2
  240.1 119.4 reduce-scatter.1
